TPU v7x, 32 devices: a whole 2x2x4 slice. The times are simulated.
32 devices in a mesh: groups: 2 (over y), store: 4 (over z), mp: 4 (over x, core).
Axes of the slice: x: 2, y: 2, z: 4, core: 2. Of those that a mesh axis runs over, the one named last changes fastest.
Arguments:
- hidden: bfloat16 [8, 128, 4096], P(('groups', 'store')), parts along dimension 0, may hold values from -6 to 6
- query_weight: bfloat16 [4096, 8192], P('store', 'mp'), may hold values from -0.09375 to 0.09375
- keyvalue_weight: bfloat16 [4096, 2048], P('store', 'mp'), may hold values from -0.09375 to 0.09375
- block_store: bfloat16 [128, 1024, 2048], P('groups', 'store', 'mp'), parts along dimension 0, may hold values from -256 to 256
- block_ids: int32 [8, 4], P('groups'), parts along dimension 0, may hold values from 0 to 63, as said below
- offsets: int32 [8, 4], P('groups'), parts along dimension 0, may hold values from 0 to 3135, as said below
- served: int32 [8], P('groups'), parts along dimension 0, may hold values from 0 to 3, each once
Outputs:
- attended: bfloat16 [8, 128, 8192], P(('groups', 'store'), None, 'mp'), parts along dimension 0
There are 2 independent parts, one for each index of `groups`. A program takes and returns all parts, laid end to end along the dimension named above; an argument that names none is the same for every part. Nothing has to cross between parts.
Inputs may be any that keep to these rules, and one draw needn't show every extreme that they name: `block_ids`: the 4 block ids of one request differ. `offsets`: block c of a request starts at c * 1024 plus 0 to 63.
All inputs are finite; a program needn't handle non-finite values.
Results may differ from a plain program's by a relative error of at most 0.004.
The roundings to bfloat16 on the way count: a program that leaves them out, or rounds other values in their place, can miss the bound.
Values may be sent and summed in bfloat16 or wider, within the bound.
A program may use at most 128 MiB of HBM per device.

v0:
```python
import math
import jax
import jax.numpy as jnp
from jax import lax
from jax.sharding import PartitionSpec as P

HD = 128
NCH = 4
L = 1024
GAP = 64


def rotary_tables(positions, head_size):
    half_size = head_size // 2
    freq_index = jnp.arange(half_size, dtype=jnp.float32)
    inverse = jnp.exp(freq_index * (-2.0 * math.log(500000.0) / head_size))
    period = jnp.floor(2.0 * math.pi / inverse + 0.5)
    position_f = positions.astype(jnp.float32)[:, None]
    angles = jnp.mod(position_f, period[None, :]) / period[None, :] * (2.0 * math.pi)
    return (jnp.cos(angles), jnp.sin(angles))


def rotate(values, cosine, sine_values):
    half_size = values.shape[-1] // 2
    first_half = values[..., :half_size]
    second_half = values[..., half_size:]
    cos_b = cosine[:, None, :]
    sin_b = sine_values[:, None, :]
    return jnp.concatenate(
        [first_half * cos_b - second_half * sin_b, second_half * cos_b + first_half * sin_b],
        axis=-1,
    )


def rerotate(page_data, positions, head_size):
    page_rows = page_data.shape[0]
    split_view = page_data.reshape(page_rows, -1, 2, head_size)
    cosine, sine_values = rotary_tables(positions, head_size)
    turned = rotate(split_view[:, :, 0, :].astype(jnp.float32), cosine, sine_values).astype(
        jnp.bfloat16
    )
    return jnp.stack([turned, split_view[:, :, 1, :]], axis=2).reshape(page_rows, -1)


def attend(queries, cached_keys, cached_values, new_keys, new_values):
    row_count = queries.shape[0]
    head_count = queries.shape[1]
    sharing = head_count // cached_keys.shape[1]
    scaling = 1.0 / math.sqrt(queries.shape[2])
    causal = jnp.arange(row_count)[:, None] >= jnp.arange(row_count)[None, :]

    def one_head(head_index):
        kv_index = head_index // sharing
        q_one = lax.dynamic_index_in_dim(queries, head_index, 1, keepdims=False)
        k_old = lax.dynamic_index_in_dim(cached_keys, kv_index, 1, keepdims=False)
        v_old = lax.dynamic_index_in_dim(cached_values, kv_index, 1, keepdims=False)
        k_new = lax.dynamic_index_in_dim(new_keys, kv_index, 1, keepdims=False)
        v_new = lax.dynamic_index_in_dim(new_values, kv_index, 1, keepdims=False)
        past_scores = jnp.dot(q_one, k_old.T, preferred_element_type=jnp.float32) * scaling
        own_scores = jnp.dot(q_one, k_new.T, preferred_element_type=jnp.float32) * scaling
        own_scores = jnp.where(causal, own_scores, -jnp.inf)
        row_top = jnp.maximum(jnp.max(past_scores, axis=1), jnp.max(own_scores, axis=1))[:, None]
        w_old = jnp.exp(past_scores - row_top)
        w_new = jnp.exp(own_scores - row_top)
        denominator = jnp.sum(w_old, axis=1) + jnp.sum(w_new, axis=1)
        mixed = jnp.dot(w_old.astype(jnp.bfloat16), v_old, preferred_element_type=jnp.float32)
        mixed = mixed + jnp.dot(
            w_new.astype(jnp.bfloat16), v_new, preferred_element_type=jnp.float32
        )
        return (mixed / denominator[:, None]).astype(jnp.bfloat16)

    per_head = lax.map(one_head, jnp.arange(head_count, dtype=jnp.int32))
    return jnp.transpose(per_head, (1, 0, 2)).reshape(row_count, head_count * queries.shape[2])


def per_device(hidden, query_weight, keyvalue_weight, block_store, block_ids, offsets, served):
    tokens = hidden[0]
    row_count = tokens.shape[0]
    q_cols = query_weight.shape[1]
    kv_cols = keyvalue_weight.shape[1]
    head_count = q_cols // HD
    kv_heads = kv_cols // (2 * HD)

    def add_rows(panel):
        return jnp.dot(tokens, panel, preferred_element_type=jnp.float32)

    my_index = lax.axis_index("store")
    slot_count = lax.axis_size("store")
    share_rows = block_store.shape[1]
    wanted = block_ids[served]
    sending = jnp.take(block_store, wanted.reshape(-1), axis=0).reshape(
        slot_count * NCH * share_rows, kv_cols
    )
    sending = sending.reshape(slot_count, NCH, share_rows, kv_cols)
    queries = add_rows(lax.all_gather(query_weight, "store", axis=0, tiled=True))
    fresh_proj = add_rows(lax.all_gather(keyvalue_weight, "store", axis=0, tiled=True))
    received = lax.all_to_all(sending, "store", split_axis=0, concat_axis=2, tiled=True)
    received = received.reshape(NCH * L, kv_cols)
    request = served[my_index]
    key_pos = (offsets[request][:, None] + jnp.arange(L, dtype=jnp.int32)[None, :]).reshape(NCH * L)
    received = rerotate(received, key_pos, HD)
    split_pages = received.reshape(NCH * L, kv_heads, 2, HD)
    query_pos = NCH * L + GAP + jnp.arange(row_count, dtype=jnp.int32)
    cos_query, sin_query = rotary_tables(query_pos, HD)
    queries = rotate(queries.reshape(row_count, head_count, HD), cos_query, sin_query).astype(
        jnp.bfloat16
    )
    fresh_proj = fresh_proj.reshape(row_count, kv_heads, 2, HD)
    new_keys = rotate(fresh_proj[:, :, 0, :], cos_query, sin_query).astype(jnp.bfloat16)
    new_values = fresh_proj[:, :, 1, :].astype(jnp.bfloat16)
    attended = attend(
        queries, split_pages[:, :, 0, :], split_pages[:, :, 1, :], new_keys, new_values
    )
    return attended[None]


def solution(mesh):
    in_specs = (
        P(("groups", "store"), None, None),
        P("store", "mp"),
        P("store", "mp"),
        P("groups", "store", "mp"),
        P("groups", None),
        P("groups", None),
        P("groups"),
    )
    out_specs = P(("groups", "store"), None, "mp")
    return jax.shard_map(
        per_device, mesh=mesh, in_specs=in_specs, out_specs=out_specs, check_vma=False
    )
```

profile of v0, /device:TPU:0, one launch (start us, length us, event | category | flops | bytes accessed | tf_op | source)
XLA Modules:
  0.0 644.8 jit_solution(6617780340946554539)
XLA Ops:
  8.7 8.5 %gather_fusion.1 = bf16[16,256,512]{2,1,0:T(8,128)(2,1)} fusion(bf16[64,256,512]{2,1,0:T(8,128)(2,1)} %param.12, s32[1024]{0:T(1024)S(1)} %pad_clamp_fusion), kind=kCustom, calls=%fused_computation.1 | custom fusion | bytes 8388672 | tf_op jit(solution)/shard_map/jit(_take)/gather | solution.py:91
  17.3 5.0 broadcast_select_fusion
  22.3 6.3 all-to-all-start
  32.3 10.7 %fusion.41 = (f32[4096,64]{1,0:T(8,128)}, f32[4096,64]{1,0:T(8,128)}) fusion(pred[64]{0:T(512)(128)(4,1)S(1)} %broadcast_compare_fusion, f32[64]{0:T(128)S(1)} %add_floor_fusion, f32[4096]{0:T(1024)S(1)} %bitcast.99), kind=kLoop, calls=%fused_computation.56 | loop fusion | flops 2359296 | bytes 2113856 | tf_op jit(solution)/shard_map/cos | solution.py:20
  43.0 124.6 %all-gather.5.cloned.1.call-done = bf16[4096,512]{1,0:T(8,128)(2,1)} async-done(((bf16[1024,512]{1,0:T(8,128)(2,1)}), bf16[4096,512]{1,0:T(8,128)(2,1)}) %all-gather.5.cloned.1.call-update) | async-done | bytes 4194320 | tf_op jit(solution)/shard_map/all_gather | solution.py:96
  167.6 6.4 copy.36
  174.0 7.6 %all-to-all-done = bf16[4,4,256,512]{3,2,1,0:T(8,128)(2,1)} async-done(((bf16[4,4,256,512]{3,2,1,0:T(8,128)(2,1)}), bf16[4,4,256,512]{3,2,1,0:T(8,128)(2,1)}, u32[]{:S(2)}, u32[]{:S(2)}) %all-to-all-start) | async-done | bytes 4194336 | tf_op jit(solution)/shard_map/all_to_all | solution.py:97
  181.6 4.9 copy.35
  186.6 7.0 %reshape_reshape.4 = bf16[4096,2,2,128]{3,2,1,0:T(2,128)(2,1)} reshape(bf16[1,4,4,256,512]{4,3,2,1,0:T(8,128)(2,1)} %copy.35) | data formatting | bytes 8388608 | tf_op jit(solution)/shard_map/reshape;reshape | solution.py:37
  193.5 8.7 %fusion.52 = (bf16[4096,2,1,128]{3,2,1,0:T(2,128)(2,1)S(1)}, f32[4096,2,1,128]{3,2,1,0:T(1,128)S(1)}) fusion(bf16[4096,2,2,128]{3,2,1,0:T(2,128)(2,1)} %reshape_reshape.4), kind=kLoop, calls=%fused_computation.91 | loop fusion | flops 1048576 | bytes 10485760 | tf_op jit(solution)/shard_map/slice | solution.py:42
  202.7 1.2 copy-done.2
  204.5 11.2 %subtract_convert_fusion = (bf16[4096,2,64]{2,1,0:T(2,128)(2,1)S(1)}, bf16[4096,2,64]{2,1,0:T(2,128)(2,1)S(1)}) fusion(f32[4096,2,128]{2,1,0:T(2,128)S(1)} %bitcast.92, f32[4096,64]{1,0:T(8,128)S(1)} %copy-done.3, f32[4096,64]{1,0:T(8,128)S(1)} %copy-done.2), kind=kLoop, calls=%fused_computation.43 | loop fusion | flops 4194304 | bytes 8388608 | tf_op jit(solution)/shard_map/convert.4
  215.7 5.7 pad_maximum_fusion
  221.4 1.6 copy.39
  223.1 1.3 copy-done.1
  224.4 1.3 fusion.36
  225.7 228.4 %all-gather.3.cloned.1.call-done = bf16[4096,2048]{1,0:T(8,128)(2,1)} async-done(((bf16[1024,2048]{1,0:T(8,128)(2,1)}), bf16[4096,2048]{1,0:T(8,128)(2,1)}) %all-gather.3.cloned.1.call-update) | async-done | bytes 16777232 | tf_op jit(solution)/shard_map/all_gather | solution.py:95
  454.1 20.7 %copy.34 = bf16[2048,4096]{1,0:T(8,128)(2,1)} copy(bf16[2048,4096]{0,1:T(8,128)(2,1)} %bitcast.94) | data formatting | bytes 33554432 | tf_op jit(solution)/shard_map/dot_general | solution.py:85
  474.8 8.1 %fusion.38 = f32[128,16,128]{0,2,1:T(8,128)S(1)} fusion(bf16[16,128,4096]{2,1,0:T(8,128)(2,1)} %bitcast.91, bf16[1,128,4096]{2,1,0:T(8,128)(2,1)S(1)} %copy-done), kind=kOutput, calls=%fused_computation.53 | convolution fusion | flops 2147483648 | bytes 18874368 | tf_op jit(solution)/shard_map/dot_general | solution.py:85
  483.9 151.7 %while.13 = (s32[]{:T(128)}, bf16[16,128,128]{2,1,0:T(8,128)(2,1)}, s32[16]{0:T(128)S(1)}, bf16[128,16,128]{0,2,1:T(8,128)(2,1)}, bf16[4096,2,128]{2,0,1:T(8,128...) while((s32[]{:T(128)}, bf16[16,128,128]{2,1,0:T(8,128)(2,1)}, ...), condition=%wide.region_5.6_spmd.clone, body=%wide.region_0.5_spmd.clone.sunk | while | flops 280149760 | bytes 8888206 | solution.py:72
  489.7 1.8 fusion.69
  498.2 1.0 fusion.70
  499.2 1.8 fusion.69
  507.7 1.0 fusion.70
  508.7 1.8 fusion.69
  517.2 1.0 fusion.70
  518.2 1.8 fusion.69
  527.6 1.8 fusion.69
  536.1 1.0 fusion.70
  537.1 1.8 fusion.69
  545.6 1.0 fusion.70
  546.6 1.8 fusion.69
  555.1 1.0 fusion.70
  556.1 1.8 fusion.69
  564.6 1.0 fusion.70
  565.6 1.8 fusion.69
  574.1 1.0 fusion.70
  575.0 1.8 fusion.69
  583.5 1.0 fusion.70
  584.5 1.8 fusion.69
  593.0 1.0 fusion.70
  594.0 1.8 fusion.69
  603.5 1.8 fusion.69
  613.0 1.8 fusion.69
  622.5 1.8 fusion.69
  631.9 1.8 fusion.69
  635.6 1.4 copy.42
  637.0 1.0 broadcast_in_dim_reshape.3
  (156 shorter events, 52.2 us)
Async XLA Ops:
  6.5 216.5 %copy-start = (bf16[1,128,4096]{2,1,0:T(8,128)(2,1)S(1)}, bf16[1,128,4096]{2,1,0:T(8,128)(2,1)}, u32[]{:S(2)}) copy-start(bf16[1,128,4096]{2,1,0:T(8,128)(2,1)} %param.9) | copy-start | bytes 3145732
  6.5 161.1 %all-gather.5.cloned.1.call-start = ((), (), s32[]{:S(2)}) async-start(), calls=%async_computation.2 | async-start | bytes 5242880 | tf_op jit(solution)/shard_map/all_gather | solution.py:96
  7.3 0.8 copy-start.5
  7.3 0.8 copy-start.4
  7.3 446.8 %all-gather.3.cloned.1.call-start = ((), (), s32[]{:S(2)}) async-start(), calls=%async_computation.1 | async-start | bytes 20971520 | tf_op jit(solution)/shard_map/all_gather | solution.py:95
  22.3 159.4 %all-to-all-start = ((bf16[4,4,256,512]{3,2,1,0:T(8,128)(2,1)}), bf16[4,4,256,512]{3,2,1,0:T(8,128)(2,1)}, u32[]{:S(2)}, u32[]{:S(2)}) async-start(bf16[4,4,256,512]{3,2,1,0:T(8,128)(2,1)} %broadcast_select_fusion), calls=%async_computation | async-start | bytes 8388608 | tf_op jit(solution)/shard_map/all_to_all | solution.py:97
  202.3 1.6 copy-start.2
  202.3 2.2 copy-start.3
  221.4 3.0 copy-start.1
Sparse Core Ops, SparseCore 0:
  8.9 158.6 all-gather.4
  169.2 284.8 all-gather.2
where the time goes:
time: 648 us; the launch traced here: 645 us
  waiting for transfers between devices  362 us (56%)
  matrix products  75.7 us (12%)
  local copies, waits for them, and re-layouts  67.7 us (10%)
  loops' own time  66.9 us (10%)
  other arithmetic  50.6 us (8%)
  between operations  15.7 us (2%)
    all_gather x1, waiting for transfers between devices, per_device(): lax.all_gather(query_weight, 'store', axis=0, tiled=True)  228 us
    all_gather x1, waiting for transfers between devices, per_device(): lax.all_gather(keyvalue_weight, 'store', axis=0, tiled=True)  125 us
    another operation x1, loops' own time, attend(): per_head = lax.map(one_head, jnp.arange(head_count, dtype=jnp.int32))  66.9 us
    dot_general x16, matrix products, one_head(): jnp.dot(q_one, k_old.T, preferred_element_type=jnp.float32) * scaling  28.6 us
    dot_general x2, local copies, waits for them, and re-layouts, add_rows(): return jnp.dot(tokens, panel, preferred_element_type=jnp.float32)  27 us
    dot_general x16, matrix products, one_head(): jnp.dot(q_one, k_new.T, preferred_element_type=jnp.float32) * scaling  15.9 us
    dot_general x16, matrix products, one_head(): jnp.dot(w_new.astype(jnp.bfloat16), v_new, preferred_element_type=jnp.flo...  13.1 us
  transfers between devices with their start and end apart: 3, of which 3 were waited for; matrix products, arithmetic and copies ran while one was open for 11% of the time, Pallas kernels for 0%

commit v1 on v0

--- a/solution.py
+++ b/solution.py
@@ -94,7 +94,12 @@
     sending = sending.reshape(slot_count, NCH, share_rows, kv_cols)
     queries = add_rows(lax.all_gather(query_weight, "store", axis=0, tiled=True))
     fresh_proj = add_rows(lax.all_gather(keyvalue_weight, "store", axis=0, tiled=True))
-    received = lax.all_to_all(sending, "store", split_axis=0, concat_axis=2, tiled=True)
+    received = jnp.concatenate(
+        lax.all_to_all(
+            jnp.stack(jnp.split(sending, lax.axis_size("store"), axis=0)), "store", 0, 0
+        ),
+        axis=2,
+    )
     received = received.reshape(NCH * L, kv_cols)
     request = served[my_index]
     key_pos = (offsets[request][:, None] + jnp.arange(L, dtype=jnp.int32)[None, :]).reshape(NCH * L)

time: 648 us -> 643 us (level)
    another operation x3 -> x4, other arithmetic: 11.3 us -> 13.6 us
  transfers between devices with their start and end apart: 3 -> 3, of which waited for: 3 -> 3; matrix products, arithmetic and copies ran while one was open for 11% -> 12% of each run, Pallas kernels for 0% -> 0%
where the time goes in v1:
time: 643 us; the launch traced here: 639 us
  waiting for transfers between devices  362 us (56%)
  matrix products  75.7 us (12%)
  local copies, waits for them, and re-layouts  66.9 us (10%)
  loops' own time  61.8 us (10%)
  other arithmetic  50.9 us (8%)
  between operations  15.6 us (2%)
    all_gather x1, waiting for transfers between devices, per_device(): lax.all_gather(query_weight, 'store', axis=0, tiled=True)  229 us
    all_gather x1, waiting for transfers between devices, per_device(): lax.all_gather(keyvalue_weight, 'store', axis=0, tiled=True)  124 us
    another operation x1, loops' own time, attend(): per_head = lax.map(one_head, jnp.arange(head_count, dtype=jnp.int32))  61.8 us
    dot_general x16, matrix products, one_head(): jnp.dot(q_one, k_old.T, preferred_element_type=jnp.float32) * scaling  28.6 us
    dot_general x2, local copies, waits for them, and re-layouts, add_rows(): return jnp.dot(tokens, panel, preferred_element_type=jnp.float32)  27.3 us
    dot_general x16, matrix products, one_head(): jnp.dot(q_one, k_new.T, preferred_element_type=jnp.float32) * scaling  15.9 us
    dot_general x16, matrix products, one_head(): jnp.dot(w_new.astype(jnp.bfloat16), v_new, preferred_element_type=jnp.flo...  13.1 us
  transfers between devices with their start and end apart: 3, of which 3 were waited for; matrix products, arithmetic and copies ran while one was open for 12% of the time, Pallas kernels for 0%

profile of v1, /device:TPU:0, one launch (start us, length us, event | category | flops | bytes accessed | tf_op | source)
XLA Modules:
  0.0 639.4 jit_solution(4198272486620178831)
XLA Ops:
  8.8 8.5 %gather_fusion.1 = bf16[16,256,512]{2,1,0:T(8,128)(2,1)} fusion(bf16[64,256,512]{2,1,0:T(8,128)(2,1)} %param.12, s32[1024]{0:T(1024)S(1)} %pad_clamp_fusion), kind=kCustom, calls=%fused_computation.1 | custom fusion | bytes 8388672 | tf_op jit(solution)/shard_map/jit(_take)/gather | solution.py:91
  17.4 3.1 broadcast_select_fusion
  20.8 2.3 pad_maximum_fusion
  23.1 6.2 all-to-all-start
  33.1 10.7 %fusion.41 = (f32[4096,64]{1,0:T(8,128)}, f32[4096,64]{1,0:T(8,128)}) fusion(pred[64]{0:T(512)(128)(4,1)S(1)} %broadcast_compare_fusion, f32[64]{0:T(128)S(1)} %add_floor_fusion, f32[4096]{0:T(1024)S(1)} %bitcast.103), kind=kLoop, calls=%fused_computation.61 | loop fusion | flops 2359296 | bytes 2113856 | tf_op jit(solution)/shard_map/cos | solution.py:20
  43.8 123.6 %all-gather.5.cloned.1.call-done = bf16[4096,512]{1,0:T(8,128)(2,1)} async-done(((bf16[1024,512]{1,0:T(8,128)(2,1)}), bf16[4096,512]{1,0:T(8,128)(2,1)}) %all-gather.5.cloned.1.call-update) | async-done | bytes 4194320 | tf_op jit(solution)/shard_map/all_gather | solution.py:96
  167.4 6.4 %copy.25 = bf16[512,4096]{1,0:T(8,128)(2,1)} copy(bf16[512,4096]{0,1:T(8,128)(2,1)} %bitcast.101) | data formatting | bytes 8388608 | tf_op jit(solution)/shard_map/dot_general | solution.py:85
  173.8 7.8 %all-to-all-done = bf16[4,1,4,256,512]{4,3,2,1,0:T(8,128)(2,1)} async-done(((bf16[4,1,4,256,512]{4,3,2,1,0:T(8,128)(2,1)}), bf16[4,1,4,256,512]{4,3,2,1,0:T(8,128)(2,1)}, u32[]{:S(2)}, u32[]{:S(2)}) %all-to-all-start) | async-done | bytes 4194336 | tf_op jit(solution)/shard_map/all_to_all | solution.py:98
  181.6 4.9 copy.24
  186.6 7.0 %reshape_reshape_reshape.3 = bf16[4096,2,2,128]{3,2,1,0:T(2,128)(2,1)} reshape(bf16[1,4,4,256,512]{4,3,2,1,0:T(8,128)(2,1)} %copy.24) | data formatting | bytes 8388608 | tf_op jit(solution)/shard_map/reshape;reshape;reshape | solution.py:37
  193.5 8.7 %fusion.52 = (bf16[4096,2,1,128]{3,2,1,0:T(2,128)(2,1)S(1)}, f32[4096,2,1,128]{3,2,1,0:T(1,128)S(1)}) fusion(bf16[4096,2,2,128]{3,2,1,0:T(2,128)(2,1)} %reshape_reshape_reshape.3), kind=kLoop, calls=%fused_computation.96 | loop fusion | flops 1048576 | bytes 10485760 | tf_op jit(solution)/shard_map/slice | solution.py:42
  202.6 1.2 copy-done.2
  204.5 11.2 %subtract_convert_fusion = (bf16[4096,2,64]{2,1,0:T(2,128)(2,1)S(1)}, bf16[4096,2,64]{2,1,0:T(2,128)(2,1)S(1)}) fusion(f32[4096,2,128]{2,1,0:T(2,128)S(1)} %bitcast.97, f32[4096,64]{1,0:T(8,128)S(1)} %copy-done.3, f32[4096,64]{1,0:T(8,128)S(1)} %copy-done.2), kind=kLoop, calls=%fused_computation.44 | loop fusion | flops 4194304 | bytes 8388608 | tf_op jit(solution)/shard_map/convert.4
  215.6 5.7 pad_maximum_fusion.1
  221.4 1.6 copy.28
  223.0 1.3 fusion.36
  224.4 229.4 %all-gather.3.cloned.1.call-done = bf16[4096,2048]{1,0:T(8,128)(2,1)} async-done(((bf16[1024,2048]{1,0:T(8,128)(2,1)}), bf16[4096,2048]{1,0:T(8,128)(2,1)}) %all-gather.3.cloned.1.call-update) | async-done | bytes 16777232 | tf_op jit(solution)/shard_map/all_gather | solution.py:95
  453.8 20.9 %copy.23 = bf16[2048,4096]{1,0:T(8,128)(2,1)} copy(bf16[2048,4096]{0,1:T(8,128)(2,1)} %bitcast.99) | data formatting | bytes 33554432 | tf_op jit(solution)/shard_map/dot_general | solution.py:85
  474.7 8.1 %fusion.38 = f32[128,16,128]{0,2,1:T(8,128)S(1)} fusion(bf16[16,128,4096]{2,1,0:T(8,128)(2,1)} %bitcast.96, bf16[1,128,4096]{2,1,0:T(8,128)(2,1)S(1)} %copy-done), kind=kOutput, calls=%fused_computation.58 | convolution fusion | flops 2147483648 | bytes 18874368 | tf_op jit(solution)/shard_map/dot_general | solution.py:85
  483.8 146.4 %while.13 = (s32[]{:T(128)}, bf16[16,128,128]{2,1,0:T(8,128)(2,1)}, s32[16]{0:T(128)S(1)}, bf16[128,16,128]{0,2,1:T(8,128)(2,1)}, bf16[4096,2,128]{2,0,1:T(8,128...) while((s32[]{:T(128)}, bf16[16,128,128]{2,1,0:T(8,128)(2,1)}, ...), condition=%wide.region_5.6_spmd.clone, body=%wide.region_0.5_spmd.clone.sunk | while | flops 280149760 | bytes 8888206 | solution.py:72
  488.3 1.0 fusion.70
  489.3 1.8 fusion.69
  497.4 1.0 fusion.70
  498.4 1.8 fusion.69
  506.6 1.0 fusion.70
  507.6 1.8 fusion.69
  515.7 1.0 fusion.70
  516.7 1.8 fusion.69
  524.9 1.0 fusion.70
  525.9 1.8 fusion.69
  534.0 1.0 fusion.70
  535.0 1.8 fusion.69
  543.2 1.0 fusion.70
  544.2 1.8 fusion.69
  552.3 1.0 fusion.70
  553.3 1.8 fusion.69
  561.5 1.0 fusion.70
  562.5 1.8 fusion.69
  570.6 1.0 fusion.70
  571.6 1.8 fusion.69
  580.8 1.8 fusion.69
  589.9 1.8 fusion.69
  599.1 1.8 fusion.69
  608.2 1.8 fusion.69
  617.4 1.8 fusion.69
  626.5 1.8 fusion.69
  630.2 1.4 copy.31
  631.6 1.0 broadcast_in_dim_reshape.3
  (159 shorter events, 52.4 us)
Async XLA Ops:
  6.5 216.5 %copy-start = (bf16[1,128,4096]{2,1,0:T(8,128)(2,1)S(1)}, bf16[1,128,4096]{2,1,0:T(8,128)(2,1)}, u32[]{:S(2)}) copy-start(bf16[1,128,4096]{2,1,0:T(8,128)(2,1)} %param.9) | copy-start | bytes 3145732
  6.5 1.5 copy-start.5
  6.5 1.5 copy-start.4
  6.5 160.8 %all-gather.5.cloned.1.call-start = ((), (), s32[]{:S(2)}) async-start(), calls=%async_computation.2 | async-start | bytes 5242880 | tf_op jit(solution)/shard_map/all_gather | solution.py:96
  7.3 446.5 %all-gather.3.cloned.1.call-start = ((), (), s32[]{:S(2)}) async-start(), calls=%async_computation.1 | async-start | bytes 20971520 | tf_op jit(solution)/shard_map/all_gather | solution.py:95
  23.1 158.5 %all-to-all-start = ((bf16[4,1,4,256,512]{4,3,2,1,0:T(8,128)(2,1)}), bf16[4,1,4,256,512]{4,3,2,1,0:T(8,128)(2,1)}, u32[]{:S(2)}, u32[]{:S(2)}) async-start(bf16[4,1,4,256,512]{4,3,2,1,0:T(8,128)(2,1)} %pad_maximum_fusion), calls=%async_computation | async-start | bytes 8388608 | tf_op jit(solution)/shard_map/all_to_all | solution.py:98
  202.2 1.6 copy-start.2
  202.2 2.2 copy-start.3
  215.6 7.4 %copy-start.1 = (bf16[512,4096]{1,0:T(8,128)(2,1)S(1)}, bf16[512,4096]{1,0:T(8,128)(2,1)}, u32[]{:S(2)}) copy-start(bf16[512,4096]{1,0:T(8,128)(2,1)} %copy.25) | copy-start | bytes 12582916
Sparse Core Ops, SparseCore 0:
  8.9 158.3 all-gather.4
  168.9 284.8 all-gather.2
